TPU v7x, 32 devices: a whole 2x2x4 slice. The times are simulated.
32 devices in a mesh: gx: 4 (over y, core), gy: 8 (over z, x).
Axes of the slice: x: 2, y: 2, z: 4, core: 2. Of those that a mesh axis runs over, the one named last changes fastest.
Arguments:
- source: float32 [256, 128, 128], P('gx', 'gy'), may hold values from -6 to 6
- diagonal: float32 [256, 128, 128], P('gx', 'gy'), may hold values from 6.05 to 7
- face_x: float32 [256, 128, 128], P('gx', 'gy'), may hold values from 0.1 to 1
- face_y: float32 [256, 128, 128], P('gx', 'gy'), may hold values from 0.1 to 1
- face_z: float32 [256, 128, 128], P('gx', 'gy'), may hold values from 0.1 to 1
- iterates: float32 [8, 256, 128, 128], P(None, 'gx', 'gy'), may hold values from -0.3 to 0.3
- labels: int32 [256, 128], P('gx', 'gy'), may hold values from 0 to 7
Outputs:
- new_iterates: float32 [8, 256, 128, 128], P(None, 'gx', 'gy')
- new_residual: float32 [256, 128, 128], P('gx', 'gy')
All inputs are finite; a program needn't handle non-finite values.
Results may differ from a plain program's by a relative error of at most 0.0003.
Values sent between devices are 32-bit elements; how exact they have to be, the bound alone decides.
No kernel may reach another device: no remote copies, remote signals or barrier semaphores. Data moves between devices by JAX's collectives and lax.ppermute only.
A program may use at most 128 MiB of HBM per device.

v0:
```python
import jax
import jax.numpy as jnp
from jax import lax
from jax.sharding import PartitionSpec as P

ENLARGE = 8
basis_shift = 6.5


def padded_2(block, sides, width):
    for axis, dim in sides:
        count = lax.axis_size(axis)
        forward = [(i, i + 1) for i in range(count - 1)]
        backward = [(target, source) for source, target in forward]
        low = lax.ppermute(
            lax.slice_in_dim(block, block.shape[dim] - width, None, axis=dim), axis, forward
        )
        high = lax.ppermute(lax.slice_in_dim(block, 0, width, axis=dim), axis, backward)
        block = jnp.concatenate([low, block, high], axis=dim)
    return block


def stencil(values, face_x, face_y, face_z, diagonal):
    centre = values[..., 1:-1, 1:-1, :]
    result = diagonal * centre
    result = (
        result
        - face_x[1:-1, 1:-1, :] * values[..., 2:, 1:-1, :]
        - face_x[:-2, 1:-1, :] * values[..., :-2, 1:-1, :]
    )
    result = (
        result
        - face_y[1:-1, 1:-1, :] * values[..., 1:-1, 2:, :]
        - face_y[1:-1, :-2, :] * values[..., 1:-1, :-2, :]
    )
    widths = [(0, 0)] * (centre.ndim - 1) + [(1, 1)]
    padded = jnp.pad(centre, widths)
    lower_face = jnp.pad(face_z[..., :-1], ((0, 0), (0, 0), (1, 0)))
    return result - face_z * padded[..., 2:] - lower_face * padded[..., :-2]


def finish(gram, project):
    highest = lax.Precision.HIGHEST
    lower = jnp.linalg.cholesky(gram)
    ident = jnp.eye(gram.shape[0], dtype=gram.dtype)
    inverse = lax.linalg.triangular_solve(lower, ident, left_side=True, lower=True)
    reduced = jnp.dot(jnp.dot(inverse, project, precision=highest), inverse.T, precision=highest)
    reduced = 0.5 * (reduced + reduced.T)
    target = jnp.dot(inverse, gram[:, :ENLARGE], precision=highest)
    factor = jnp.linalg.cholesky(reduced)
    middle = lax.linalg.triangular_solve(factor, target, left_side=True, lower=True)
    solved = lax.linalg.triangular_solve(
        factor, middle, left_side=True, lower=True, transpose_a=True
    )
    return jnp.dot(inverse.T, solved, precision=highest)


def shards(source, diagonal, face_x, face_y, face_z, iterates, labels):
    highest = lax.Precision.HIGHEST
    summed = jnp.sum(iterates, axis=0)
    columns = jnp.arange(ENLARGE, dtype=jnp.int32)
    near = (
        padded_2(summed, (("gx", 0), ("gy", 1)), 1),
        padded_2(face_x, (("gx", 0), ("gy", 1)), 1),
        padded_2(face_y, (("gx", 0), ("gy", 1)), 1),
    )
    near_sum, near_fx, near_fy = near
    residual = source - stencil(near_sum, near_fx, near_fy, face_z, diagonal)
    onehot = (labels[None] == columns[:, None, None]).astype(jnp.float32)
    blocks = residual[None] * onehot[..., None]
    blocks_wide = padded_2(blocks, (("gx", 1), ("gy", 2)), 1)
    applied = stencil(blocks_wide, near_fx, near_fy, face_z, diagonal)
    powered = applied - basis_shift * blocks
    powered_wide = padded_2(powered, (("gx", 1), ("gy", 2)), 1)
    second = stencil(powered_wide, near_fx, near_fy, face_z, diagonal)
    basis = jnp.concatenate([blocks, powered], axis=0)
    image = jnp.concatenate([applied, second], axis=0)
    gram_local = jnp.einsum("aijk,bijk->ab", basis, basis, precision=highest)
    project_local = jnp.einsum("aijk,bijk->ab", basis, image, precision=highest)
    gram = lax.psum(gram_local, ("gx", "gy"))
    project = lax.psum(project_local, ("gx", "gy"))
    coeffs = finish(gram, project)
    new_iterates = iterates + jnp.einsum("ab,aijk->bijk", coeffs, basis, precision=highest)
    carried = jnp.sum(coeffs, axis=1)
    new_residual = residual - jnp.einsum("a,aijk->ijk", carried, image, precision=highest)
    return (new_iterates, new_residual)


def solution(mesh):
    placed = (
        P("gx", "gy", None),
        P("gx", "gy", None),
        P("gx", "gy", None),
        P("gx", "gy", None),
        P("gx", "gy", None),
        P(None, "gx", "gy", None),
        P("gx", "gy"),
    )
    return jax.shard_map(
        shards,
        mesh=mesh,
        in_specs=placed,
        out_specs=(P(None, "gx", "gy", None), P("gx", "gy", None)),
        check_vma=False,
    )
```

profile of v0, /device:TPU:0, one launch (start us, length us, event | category | flops | bytes accessed | tf_op | source)
XLA Modules:
  0.0 177.3 jit_solution(15040397435094770270)
XLA Ops:
  0.7 2.7 %reduce_sum.18 = f32[64,16,128]{2,1,0:T(8,128)S(1)} reduce(f32[8,64,16,128]{3,2,1,0:T(8,128)} %param.13, f32[]{:T(128)} %constant.43.clone.1), dimensions={0}, to_apply=%region_0.0 | reduce | flops 917504 | bytes 4718596 | tf_op jit(solution)/shard_map/reduce_sum | solution.py:60
  3.4 1.3 collective-permute-start
  4.7 3.0 %collective-permute-start.2 = (f32[1,16,128]{2,1,0:T(8,128)S(1)}, f32[1,16,128]{2,1,0:T(8,128)S(1)}, u32[]{:S(2)}, u32[]{:S(2)}) collective-permute-start(f32[1,16,128]{2,1,0:T(8,128)S(1)} %get-tuple-element.23), channel_id=1, source_target_pairs={{0,8},{8,16},{16,24},{1,9},{9,17},{17,25},{2,10},{10,18},{18,26},{... | collective-permute-start | bytes 24584 | tf_op jit(solution)/shard_map/ppermute | solution.py:15
  7.7 4.5 %collective-permute-start.4 = (f32[1,16,128]{2,1,0:T(8,128)S(1)}, f32[1,16,128]{2,1,0:T(8,128)S(1)}, u32[]{:S(2)}, u32[]{:S(2)}) collective-permute-start(f32[1,16,128]{2,1,0:T(8,128)S(1)} %get-tuple-element.22), channel_id=1, source_target_pairs={{0,8},{8,16},{16,24},{1,9},{9,17},{17,25},{2,10},{10,18},{18,26},{... | collective-permute-start | bytes 24584 | tf_op jit(solution)/shard_map/ppermute | solution.py:15
  12.2 1.3 collective-permute-start.5
  13.6 3.0 %collective-permute-start.1 = (f32[1,16,128]{2,1,0:T(8,128)S(1)}, f32[1,16,128]{2,1,0:T(8,128)S(1)}, u32[]{:S(2)}, u32[]{:S(2)}) collective-permute-start(f32[1,16,128]{2,1,0:T(8,128)S(1)} %slice.156), channel_id=1, source_target_pairs={{0,8},{8,16},{16,24},{1,9},{9,17},{17,25},{2,10},{10,18},{18,26},{... | collective-permute-start | bytes 24584 | tf_op jit(solution)/shard_map/ppermute | solution.py:15
  16.8 1.3 collective-permute-start.3
  18.1 4.5 %collective-permute-start.7 = (f32[66,1,128]{2,1,0:T(1,128)S(1)}, f32[66,1,128]{2,1,0:T(1,128)S(1)}, u32[]{:S(2)}, u32[]{:S(2)}) collective-permute-start(f32[66,1,128]{2,1,0:T(1,128)S(1)} %get-tuple-element.20), channel_id=1, source_target_pairs={{0,1},{1,2},{2,3},{3,4},{4,5},{5,6},{6,7},{8,9},{9,10},{10,11},{11... | collective-permute-start | bytes 101384 | tf_op jit(solution)/shard_map/ppermute | solution.py:15
  22.7 4.3 %collective-permute-start.6 = (f32[66,1,128]{2,1,0:T(1,128)S(1)}, f32[66,1,128]{2,1,0:T(1,128)S(1)}, u32[]{:S(2)}, u32[]{:S(2)}) collective-permute-start(f32[66,1,128]{2,1,0:T(1,128)S(1)} %slice.194), channel_id=1, source_target_pairs={{0,1},{1,2},{2,3},{3,4},{4,5},{5,6},{6,7},{8,9},{9,10},{10,11},{11... | collective-permute-start | bytes 101384 | tf_op jit(solution)/shard_map/ppermute | solution.py:15
  27.3 1.3 collective-permute-done.6
  28.6 1.6 fusion.33
  31.5 1.3 collective-permute-start.8
  32.8 3.0 %collective-permute-start.9 = (f32[8,1,16,128]{3,0,2,1:T(8,128)S(1)}, f32[8,1,16,128]{3,0,2,1:T(8,128)S(1)}, u32[]{:S(2)}, u32[]{:S(2)}) collective-permute-start(f32[8,1,16,128]{3,0,2,1:T(8,128)S(1)} %get-tuple-element.17), channel_id=1, source_target_pairs={{0,8},{8,16},{16,24},{1,9},{9,17},{17,25},{2,10},{10,18},{18,26},{... | collective-permute-start | bytes 196616 | tf_op jit(solution)/shard_map/ppermute | solution.py:15
  36.8 1.3 collective-permute-start.10
  38.1 5.0 %collective-permute-start.11 = (f32[8,66,1,128]{3,0,2,1:T(8,128)S(1)}, f32[8,66,1,128]{3,0,2,1:T(8,128)S(1)}, u32[]{:S(2)}, u32[]{:S(2)}) collective-permute-start(f32[8,66,1,128]{3,0,2,1:T(8,128)S(1)} %get-tuple-element.14), channel_id=1, source_target_pairs={{0,1},{1,2},{2,3},{3,4},{4,5},{5,6},{6,7},{8,9},{9,10},{10,11},{11... | collective-permute-start | bytes 811016 | tf_op jit(solution)/shard_map/ppermute | solution.py:15
  43.4 4.0 %collective-permute-done.10 = f32[8,66,1,128]{3,0,2,1:T(8,128)S(1)} collective-permute-done((f32[8,66,1,128]{3,0,2,1:T(8,128)S(1)}, f32[8,66,1,128]{3,0,2,1:T(8,128)S(1)}, u32[]{:S(2)}, u32[]{:S(2)}) %collective-permute-start.10) | collective-permute-done | bytes 270368 | tf_op jit(solution)/shard_map/ppermute | solution.py:18
  47.4 7.2 %collective-permute-done.11 = f32[8,66,1,128]{3,0,2,1:T(8,128)S(1)} collective-permute-done((f32[8,66,1,128]{3,0,2,1:T(8,128)S(1)}, f32[8,66,1,128]{3,0,2,1:T(8,128)S(1)}, u32[]{:S(2)}, u32[]{:S(2)}) %collective-permute-start.11) | collective-permute-done | bytes 270368 | tf_op jit(solution)/shard_map/ppermute | solution.py:15
  54.6 7.5 %multiply_subtract_fusion = (f32[8,64,16,128]{3,0,2,1:T(8,128)S(1)}, f32[8,64,16,128]{3,0,2,1:T(8,128)S(1)}) fusion(f32[8,64,16]{0,2,1:T(8,128)S(1)} %fusion.43, f32[64,16,128]{2,1,0:T(8,128)S(1)} %get-tuple-element.9, f32[64,16,128]{2,1,0:T(8,128)S(1)} %pad.18, f32[8,64,16,128]{3,0,2,1:T(8,128)S(1)} %broadcast_multiply_fusion, ...), kind=kLoop, calls=%fused_computation.51 | loop fusion | flops 25165824 | bytes 17481728 | tf_op jit(solution)/shard_map/sub | solution.py:73
  62.1 1.3 collective-permute-start.12
  63.4 3.0 %collective-permute-start.13 = (f32[8,1,16,128]{3,0,2,1:T(8,128)S(1)}, f32[8,1,16,128]{3,0,2,1:T(8,128)S(1)}, u32[]{:S(2)}, u32[]{:S(2)}) collective-permute-start(f32[8,1,16,128]{3,0,2,1:T(8,128)S(1)} %get-tuple-element.15), channel_id=1, source_target_pairs={{0,8},{8,16},{16,24},{1,9},{9,17},{17,25},{2,10},{10,18},{18,26},{... | collective-permute-start | bytes 196616 | tf_op jit(solution)/shard_map/ppermute | solution.py:15
  67.4 1.3 collective-permute-start.14
  68.7 5.0 %collective-permute-start.15 = (f32[8,66,1,128]{3,0,2,1:T(8,128)S(1)}, f32[8,66,1,128]{3,0,2,1:T(8,128)S(1)}, u32[]{:S(2)}, u32[]{:S(2)}) collective-permute-start(f32[8,66,1,128]{3,0,2,1:T(8,128)S(1)} %get-tuple-element.12), channel_id=1, source_target_pairs={{0,1},{1,2},{2,3},{3,4},{4,5},{5,6},{6,7},{8,9},{9,10},{10,11},{11... | collective-permute-start | bytes 811016 | tf_op jit(solution)/shard_map/ppermute | solution.py:15
  73.7 11.2 %fusion.28 = f32[16,16]{0,1:T(8,128)S(1)} fusion(f32[8,64,16,128]{3,0,2,1:T(8,128)S(1)} %get-tuple-element.7, f32[8,64,16,128]{3,0,2,1:T(8,128)S(1)} %broadcast_multiply_fusion), kind=kOutput, calls=%fused_computation.55 | convolution fusion | flops 404750336 | bytes 8389632 | tf_op jit(solution)/shard_map/aijk,bijk->ab/dot_general | solution.py:78
  85.3 6.8 %fusion.10 = f32[8,64,16,128]{3,0,2,1:T(8,128)S(1)} fusion(f32[8,64,16,128]{3,0,2,1:T(8,128)S(1)} %get-tuple-element.7, f32[8,66,1,128]{3,0,2,1:T(8,128)S(1)} %collective-permute-done.15, f32[8,1,16,128]{3,0,2,1:T(8,128)S(1)} %collective-permute-done.12, f32[8,1,16,128]{3,0,2,1:T(8,128)S(1)} %collective-permute-done.13, ...), kind=kLoop, calls=%fused_computation.16 | loop fusion | flops 22020096 | bytes 12730368 | tf_op jit(solution)/shard_map/sub | solution.py:39
  92.1 1.9 %copy-done.5 = f32[8,64,16,128]{3,0,2,1:T(8,128)} copy-done((f32[8,64,16,128]{3,0,2,1:T(8,128)}, f32[8,64,16,128]{3,0,2,1:T(8,128)S(1)}, u32[]{:S(2)}) %copy-start.5) | copy-done | bytes 4194328
  94.1 10.4 %fusion.29 = f32[16,16]{1,0:T(8,128)S(1)} fusion(f32[8,64,16,128]{3,0,2,1:T(8,128)S(1)} %fusion.10, f32[8,64,16,128]{3,0,2,1:T(8,128)S(1)} %get-tuple-element.8, f32[8,64,16,128]{3,0,2,1:T(8,128)S(1)} %get-tuple-element.7, f32[8,64,16,128]{3,0,2,1:T(8,128)S(1)} %broadcast_multiply_fusion), kind=kOutput, calls=%fused_computation.56 | convolution fusion | flops 406847488 | bytes 16778240 | tf_op jit(solution)/shard_map/aijk,bijk->ab/dot_general | solution.py:79
  104.5 44.6 %all-reduce.4 = (f32[16,16]{0,1:T(8,128)S(1)}, f32[16,16]{1,0:T(8,128)S(1)}) all-reduce(f32[16,16]{0,1:T(8,128)S(1)} %fusion.28, f32[16,16]{1,0:T(8,128)S(1)} %fusion.29), channel_id=1, replica_groups=mesh['gx'=4,'gy'=8] {'gx','gy'}, use_global_device_ids=true, to_apply=%region_1.2 | all-reduce | flops 512 | bytes 4096 | tf_op jit(solution)/shard_map/psum | solution.py:80
  149.1 1.5 cholesky.44
  153.9 1.5 cholesky.55
  158.5 6.6 %fusion = f32[1,64,16,128]{3,0,2,1:T(1,128)S(1)} fusion(f32[8,64,16,128]{3,0,2,1:T(8,128)} %copy-done.5, f32[8,64,16,128]{3,0,2,1:T(8,128)} %copy-done.4, f32[16]{0:T(128)S(1)} %get-tuple-element.25), kind=kOutput, calls=%fused_computation.6 | convolution fusion | flops 27262976 | bytes 8912960 | tf_op jit(solution)/shard_map/a,aijk->ijk/dot_general | solution.py:85
  166.0 8.6 %copy_add_fusion = f32[8,64,16,128]{3,0,2,1:T(8,128)S(1)} fusion(f32[8,64,16,128]{3,2,1,0:T(8,128)} %param.13, f32[8,64,16,128]{3,0,2,1:T(8,128)S(1)} %copy-done.3, f32[8,64,16,128]{3,0,2,1:T(8,128)S(1)} %copy-done.1, f32[16,8]{0,1:T(8,128)S(1)} %get-tuple-element.26), kind=kOutput, calls=%fused_computation.50 | convolution fusion | flops 204472320 | bytes 16777728 | tf_op jit(solution)/shard_map/ab,aijk->bijk/dot_general | solution.py:83
  174.6 2.8 %copy.15 = f32[8,64,16,128]{3,2,1,0:T(8,128)} copy(f32[8,64,16,128]{3,0,2,1:T(8,128)S(1)} %copy_add_fusion) | data formatting | bytes 8388608
  (73 shorter events, 11.6 us)
Async XLA Ops:
  0.6 7.1 %copy-start.7 = (f32[64,16,128]{2,1,0:T(8,128)S(1)}, f32[64,16,128]{2,1,0:T(8,128)}, u32[]{:S(2)}) copy-start(f32[64,16,128]{2,1,0:T(8,128)} %param.11) | copy-start | bytes 1572868
  0.6 12.9 %copy-start.8 = (f32[64,16,128]{2,1,0:T(8,128)S(1)}, f32[64,16,128]{2,1,0:T(8,128)}, u32[]{:S(2)}) copy-start(f32[64,16,128]{2,1,0:T(8,128)} %param.10) | copy-start | bytes 1572868
  0.7 15.9 %copy-start.10 = (s32[64,16]{0,1:T(8,128)S(1)}, s32[64,16]{0,1:T(8,128)}, u32[]{:S(2)}) copy-start(s32[64,16]{0,1:T(8,128)} %param.14) | copy-start | bytes 12292
  0.7 28.0 %copy-start.6 = (f32[64,16,128]{2,1,0:T(8,128)S(1)}, f32[64,16,128]{2,1,0:T(8,128)}, u32[]{:S(2)}) copy-start(f32[64,16,128]{2,1,0:T(8,128)} %param.12) | copy-start | bytes 1572868
  0.7 28.0 %copy-start.9 = (f32[64,16,128]{2,1,0:T(8,128)S(1)}, f32[64,16,128]{2,1,0:T(8,128)}, u32[]{:S(2)}) copy-start(f32[64,16,128]{2,1,0:T(8,128)} %param.9) | copy-start | bytes 1572868
  3.4 13.3 %collective-permute-start = (f32[1,16,128]{2,1,0:T(8,128)S(1)}, f32[1,16,128]{2,1,0:T(8,128)S(1)}, u32[]{:S(2)}, u32[]{:S(2)}) collective-permute-start(f32[1,16,128]{2,1,0:T(8,128)S(1)} %get-tuple-element.24), channel_id=1, source_target_pairs={{8,0},{16,8},{24,16},{9,1},{17,9},{25,17},{10,2},{18,10},{26,18},{... | collective-permute-start | bytes 24584 | tf_op jit(solution)/shard_map/ppermute | solution.py:18
  4.7 12.0 %collective-permute-start.2 = (f32[1,16,128]{2,1,0:T(8,128)S(1)}, f32[1,16,128]{2,1,0:T(8,128)S(1)}, u32[]{:S(2)}, u32[]{:S(2)}) collective-permute-start(f32[1,16,128]{2,1,0:T(8,128)S(1)} %get-tuple-element.23), channel_id=1, source_target_pairs={{0,8},{8,16},{16,24},{1,9},{9,17},{17,25},{2,10},{10,18},{18,26},{... | collective-permute-start | bytes 24584 | tf_op jit(solution)/shard_map/ppermute | solution.py:15
  7.7 14.9 %collective-permute-start.4 = (f32[1,16,128]{2,1,0:T(8,128)S(1)}, f32[1,16,128]{2,1,0:T(8,128)S(1)}, u32[]{:S(2)}, u32[]{:S(2)}) collective-permute-start(f32[1,16,128]{2,1,0:T(8,128)S(1)} %get-tuple-element.22), channel_id=1, source_target_pairs={{0,8},{8,16},{16,24},{1,9},{9,17},{17,25},{2,10},{10,18},{18,26},{... | collective-permute-start | bytes 24584 | tf_op jit(solution)/shard_map/ppermute | solution.py:15
  12.2 10.4 %collective-permute-start.5 = (f32[1,16,128]{2,1,0:T(8,128)S(1)}, f32[1,16,128]{2,1,0:T(8,128)S(1)}, u32[]{:S(2)}, u32[]{:S(2)}) collective-permute-start(f32[1,16,128]{2,1,0:T(8,128)S(1)} %get-tuple-element.21), channel_id=1, source_target_pairs={{8,0},{16,8},{24,16},{9,1},{17,9},{25,17},{10,2},{18,10},{26,18},{... | collective-permute-start | bytes 24584 | tf_op jit(solution)/shard_map/ppermute | solution.py:18
  13.6 13.7 %collective-permute-start.1 = (f32[1,16,128]{2,1,0:T(8,128)S(1)}, f32[1,16,128]{2,1,0:T(8,128)S(1)}, u32[]{:S(2)}, u32[]{:S(2)}) collective-permute-start(f32[1,16,128]{2,1,0:T(8,128)S(1)} %slice.156), channel_id=1, source_target_pairs={{0,8},{8,16},{16,24},{1,9},{9,17},{17,25},{2,10},{10,18},{18,26},{... | collective-permute-start | bytes 24584 | tf_op jit(solution)/shard_map/ppermute | solution.py:15
  16.8 10.5 %collective-permute-start.3 = (f32[66,1,128]{2,1,0:T(1,128)S(1)}, f32[66,1,128]{2,1,0:T(1,128)S(1)}, u32[]{:S(2)}, u32[]{:S(2)}) collective-permute-start(f32[66,1,128]{2,1,0:T(1,128)S(1)} %get-tuple-element.19), channel_id=1, source_target_pairs={{1,0},{2,1},{3,2},{4,3},{5,4},{6,5},{7,6},{9,8},{10,9},{11,10},{12... | collective-permute-start | bytes 101384 | tf_op jit(solution)/shard_map/ppermute | solution.py:18
  18.1 9.2 %collective-permute-start.7 = (f32[66,1,128]{2,1,0:T(1,128)S(1)}, f32[66,1,128]{2,1,0:T(1,128)S(1)}, u32[]{:S(2)}, u32[]{:S(2)}) collective-permute-start(f32[66,1,128]{2,1,0:T(1,128)S(1)} %get-tuple-element.20), channel_id=1, source_target_pairs={{0,1},{1,2},{2,3},{3,4},{4,5},{5,6},{6,7},{8,9},{9,10},{10,11},{11... | collective-permute-start | bytes 101384 | tf_op jit(solution)/shard_map/ppermute | solution.py:15
  22.7 5.9 %collective-permute-start.6 = (f32[66,1,128]{2,1,0:T(1,128)S(1)}, f32[66,1,128]{2,1,0:T(1,128)S(1)}, u32[]{:S(2)}, u32[]{:S(2)}) collective-permute-start(f32[66,1,128]{2,1,0:T(1,128)S(1)} %slice.194), channel_id=1, source_target_pairs={{0,1},{1,2},{2,3},{3,4},{4,5},{5,6},{6,7},{8,9},{9,10},{10,11},{11... | collective-permute-start | bytes 101384 | tf_op jit(solution)/shard_map/ppermute | solution.py:15
  31.5 60.6 %copy-start = (f32[8,64,16,128]{3,0,2,1:T(8,128)}, f32[8,64,16,128]{3,0,2,1:T(8,128)S(1)}, u32[]{:S(2)}) copy-start(f32[8,64,16,128]{3,0,2,1:T(8,128)S(1)} %broadcast_multiply_fusion) | copy-start | bytes 12582916
  31.5 4.3 %collective-permute-start.8 = (f32[8,1,16,128]{3,0,2,1:T(8,128)S(1)}, f32[8,1,16,128]{3,0,2,1:T(8,128)S(1)}, u32[]{:S(2)}, u32[]{:S(2)}) collective-permute-start(f32[8,1,16,128]{3,0,2,1:T(8,128)S(1)} %get-tuple-element.18), channel_id=1, source_target_pairs={{8,0},{16,8},{24,16},{9,1},{17,9},{25,17},{10,2},{18,10},{26,18},{... | collective-permute-start | bytes 196616 | tf_op jit(solution)/shard_map/ppermute | solution.py:18
  32.8 3.9 %collective-permute-start.9 = (f32[8,1,16,128]{3,0,2,1:T(8,128)S(1)}, f32[8,1,16,128]{3,0,2,1:T(8,128)S(1)}, u32[]{:S(2)}, u32[]{:S(2)}) collective-permute-start(f32[8,1,16,128]{3,0,2,1:T(8,128)S(1)} %get-tuple-element.17), channel_id=1, source_target_pairs={{0,8},{8,16},{16,24},{1,9},{9,17},{17,25},{2,10},{10,18},{18,26},{... | collective-permute-start | bytes 196616 | tf_op jit(solution)/shard_map/ppermute | solution.py:15
  36.8 10.6 %collective-permute-start.10 = (f32[8,66,1,128]{3,0,2,1:T(8,128)S(1)}, f32[8,66,1,128]{3,0,2,1:T(8,128)S(1)}, u32[]{:S(2)}, u32[]{:S(2)}) collective-permute-start(f32[8,66,1,128]{3,0,2,1:T(8,128)S(1)} %get-tuple-element.13), channel_id=1, source_target_pairs={{1,0},{2,1},{3,2},{4,3},{5,4},{6,5},{7,6},{9,8},{10,9},{11,10},{12... | collective-permute-start | bytes 811016 | tf_op jit(solution)/shard_map/ppermute | solution.py:18
  38.1 16.6 %collective-permute-start.11 = (f32[8,66,1,128]{3,0,2,1:T(8,128)S(1)}, f32[8,66,1,128]{3,0,2,1:T(8,128)S(1)}, u32[]{:S(2)}, u32[]{:S(2)}) collective-permute-start(f32[8,66,1,128]{3,0,2,1:T(8,128)S(1)} %get-tuple-element.14), channel_id=1, source_target_pairs={{0,1},{1,2},{2,3},{3,4},{4,5},{5,6},{6,7},{8,9},{9,10},{10,11},{11... | collective-permute-start | bytes 811016 | tf_op jit(solution)/shard_map/ppermute | solution.py:15
  62.1 30.0 %copy-start.2 = (f32[8,64,16,128]{3,0,2,1:T(8,128)}, f32[8,64,16,128]{3,0,2,1:T(8,128)S(1)}, u32[]{:S(2)}) copy-start(f32[8,64,16,128]{3,0,2,1:T(8,128)S(1)} %get-tuple-element.7) | copy-start | bytes 12582916
  62.1 30.0 %copy-start.4 = (f32[8,64,16,128]{3,0,2,1:T(8,128)}, f32[8,64,16,128]{3,0,2,1:T(8,128)S(1)}, u32[]{:S(2)}) copy-start(f32[8,64,16,128]{3,0,2,1:T(8,128)S(1)} %get-tuple-element.8) | copy-start | bytes 12582916
  62.1 4.3 %collective-permute-start.12 = (f32[8,1,16,128]{3,0,2,1:T(8,128)S(1)}, f32[8,1,16,128]{3,0,2,1:T(8,128)S(1)}, u32[]{:S(2)}, u32[]{:S(2)}) collective-permute-start(f32[8,1,16,128]{3,0,2,1:T(8,128)S(1)} %get-tuple-element.16), channel_id=1, source_target_pairs={{8,0},{16,8},{24,16},{9,1},{17,9},{25,17},{10,2},{18,10},{26,18},{... | collective-permute-start | bytes 196616 | tf_op jit(solution)/shard_map/ppermute | solution.py:18
  63.4 3.9 %collective-permute-start.13 = (f32[8,1,16,128]{3,0,2,1:T(8,128)S(1)}, f32[8,1,16,128]{3,0,2,1:T(8,128)S(1)}, u32[]{:S(2)}, u32[]{:S(2)}) collective-permute-start(f32[8,1,16,128]{3,0,2,1:T(8,128)S(1)} %get-tuple-element.15), channel_id=1, source_target_pairs={{0,8},{8,16},{16,24},{1,9},{9,17},{17,25},{2,10},{10,18},{18,26},{... | collective-permute-start | bytes 196616 | tf_op jit(solution)/shard_map/ppermute | solution.py:15
  67.4 17.5 %collective-permute-start.14 = (f32[8,66,1,128]{3,0,2,1:T(8,128)S(1)}, f32[8,66,1,128]{3,0,2,1:T(8,128)S(1)}, u32[]{:S(2)}, u32[]{:S(2)}) collective-permute-start(f32[8,66,1,128]{3,0,2,1:T(8,128)S(1)} %get-tuple-element.11), channel_id=1, source_target_pairs={{1,0},{2,1},{3,2},{4,3},{5,4},{6,5},{7,6},{9,8},{10,9},{11,10},{12... | collective-permute-start | bytes 811016 | tf_op jit(solution)/shard_map/ppermute | solution.py:18
  68.7 16.6 %collective-permute-start.15 = (f32[8,66,1,128]{3,0,2,1:T(8,128)S(1)}, f32[8,66,1,128]{3,0,2,1:T(8,128)S(1)}, u32[]{:S(2)}, u32[]{:S(2)}) collective-permute-start(f32[8,66,1,128]{3,0,2,1:T(8,128)S(1)} %get-tuple-element.12), channel_id=1, source_target_pairs={{0,1},{1,2},{2,3},{3,4},{4,5},{5,6},{6,7},{8,9},{9,10},{10,11},{11... | collective-permute-start | bytes 811016 | tf_op jit(solution)/shard_map/ppermute | solution.py:15
  92.1 2.0 %copy-start.5 = (f32[8,64,16,128]{3,0,2,1:T(8,128)}, f32[8,64,16,128]{3,0,2,1:T(8,128)S(1)}, u32[]{:S(2)}) copy-start(f32[8,64,16,128]{3,0,2,1:T(8,128)S(1)} %fusion.10) | copy-start | bytes 12582916
  158.5 7.5 %copy-start.1 = (f32[8,64,16,128]{3,0,2,1:T(8,128)S(1)}, f32[8,64,16,128]{3,0,2,1:T(8,128)}, u32[]{:S(2)}) copy-start(f32[8,64,16,128]{3,0,2,1:T(8,128)} %copy-done) | copy-start | bytes 12582916
  158.5 7.5 %copy-start.3 = (f32[8,64,16,128]{3,0,2,1:T(8,128)S(1)}, f32[8,64,16,128]{3,0,2,1:T(8,128)}, u32[]{:S(2)}) copy-start(f32[8,64,16,128]{3,0,2,1:T(8,128)} %copy-done.2) | copy-start | bytes 12582916
where the time goes:
time: 178 us; the launch traced here: 177 us
  starting transfers between devices  44.6 us (25%)
  blocking collectives  44.6 us (25%)
  matrix products  37.9 us (21%)
  other arithmetic  29 us (16%)
  waiting for transfers between devices  14.8 us (8%)
  local copies, waits for them, and re-layouts  5.36 us (3%)
    psum x1, blocking collectives, shards(): gram = lax.psum(gram_local, ('gx', 'gy'))  44.6 us
    ppermute x9, starting transfers between devices, padded_2(): lax.ppermute(lax.slice_in_dim(block, block.shape[dim] - width, None, axis...  35.5 us
    dot_general x1, matrix products, shards(): gram_local = jnp.einsum('aijk,bijk->ab', basis, basis, precision=highest)  11.2 us
    ppermute x9, waiting for transfers between devices, padded_2(): lax.ppermute(lax.slice_in_dim(block, block.shape[dim] - width, None, axis...  10.7 us
    dot_general x1, matrix products, shards(): project_local = jnp.einsum('aijk,bijk->ab', basis, image, precision=highest)  10.4 us
    ppermute x7, starting transfers between devices, padded_2(): lax.ppermute(lax.slice_in_dim(block, 0, width, axis=dim), axis, backward)  9.04 us
    dot_general x1, matrix products, shards(): jnp.einsum('ab,aijk->bijk', coeffs, basis, precision=highest)  8.56 us
    sub x1, other arithmetic, shards(): powered = applied - basis_shift * blocks  7.45 us
  transfers between devices with their start and end apart: 16, of which 6 were waited for; matrix products, arithmetic and copies ran while one was open for 7% of the time, Pallas kernels for 0%

commit v1 on v0

--- a/solution.py
+++ b/solution.py
@@ -77,7 +77,7 @@
     image = jnp.concatenate([applied, second], axis=0)
     gram_local = jnp.einsum("aijk,bijk->ab", basis, basis, precision=highest)
     project_local = jnp.einsum("aijk,bijk->ab", basis, image, precision=highest)
-    gram = lax.psum(gram_local, ("gx", "gy"))
+    gram = jax.lax.psum(jax.lax.psum(gram_local, "gy"), "gx")
     project = lax.psum(project_local, ("gx", "gy"))
     coeffs = finish(gram, project)
     new_iterates = iterates + jnp.einsum("ab,aijk->bijk", coeffs, basis, precision=highest)

time: 178 us -> 208 us (1.17)
  blocking collectives: 44.6 us -> 64.8 us
  waiting for transfers between devices: 14.8 us -> 20.8 us
  other arithmetic: 29 us -> 32.1 us
    psum x1 -> x3, blocking collectives: 44.6 us -> 64.8 us  [the longest x1 38.9 us: shards(): project = lax.psum(project_local, ('gx', 'gy'))]
    ppermute x7, waiting for transfers between devices: 4.06 us -> 7.78 us  [padded_2(): lax.ppermute(lax.slice_in_dim(block, 0, width, axis=dim), axis, backward)]
    ppermute x9, waiting for transfers between devices: 10.7 us -> 13.1 us  [padded_2(): lax.ppermute(lax.slice_in_dim(block, block.shape[dim] - width, None, axis...]
    unnamed x26 -> x36, local copies, waits for them, and re-layouts: 4.88 us -> 4.92 us
  transfers between devices with their start and end apart: 16 -> 16, of which waited for: 6 -> 6; matrix products, arithmetic and copies ran while one was open for 7% -> 2% of each run, Pallas kernels for 0% -> 0%
where the time goes in v1:
time: 208 us; the launch traced here: 207 us
  blocking collectives  64.8 us (31%)
  starting transfers between devices  44.6 us (21%)
  matrix products  38.1 us (18%)
  other arithmetic  32.1 us (15%)
  waiting for transfers between devices  20.8 us (10%)
  local copies, waits for them, and re-layouts  5.41 us (3%)
    psum x1, blocking collectives, shards(): project = lax.psum(project_local, ('gx', 'gy'))  38.9 us
    ppermute x9, starting transfers between devices, padded_2(): lax.ppermute(lax.slice_in_dim(block, block.shape[dim] - width, None, axis...  35.1 us
    psum x2, blocking collectives, shards(): gram = jax.lax.psum(jax.lax.psum(gram_local, 'gy'), 'gx')  25.9 us
    ppermute x9, waiting for transfers between devices, padded_2(): lax.ppermute(lax.slice_in_dim(block, block.shape[dim] - width, None, axis...  13.1 us
    dot_general x1, matrix products, shards(): gram_local = jnp.einsum('aijk,bijk->ab', basis, basis, precision=highest)  11.2 us
    dot_general x1, matrix products, shards(): project_local = jnp.einsum('aijk,bijk->ab', basis, image, precision=highest)  10.6 us
    ppermute x7, starting transfers between devices, padded_2(): lax.ppermute(lax.slice_in_dim(block, 0, width, axis=dim), axis, backward)  9.5 us
    dot_general x1, matrix products, shards(): jnp.einsum('ab,aijk->bijk', coeffs, basis, precision=highest)  8.55 us
  transfers between devices with their start and end apart: 16, of which 6 were waited for; matrix products, arithmetic and copies ran while one was open for 2% of the time, Pallas kernels for 0%

profile of v1, /device:TPU:0, one launch (start us, length us, event | category | flops | bytes accessed | tf_op | source)
XLA Modules:
  0.0 206.9 jit_solution(9376727739147043314)
XLA Ops:
  0.7 2.7 %reduce_sum.18 = f32[64,16,128]{2,1,0:T(8,128)S(1)} reduce(f32[8,64,16,128]{3,2,1,0:T(8,128)} %param.13, f32[]{:T(128)} %constant.43.clone.1), dimensions={0}, to_apply=%region_0.0 | reduce | flops 917504 | bytes 4718596 | tf_op jit(solution)/shard_map/reduce_sum | solution.py:60
  4.7 3.0 %collective-permute-start.2 = (f32[1,16,128]{2,1,0:T(8,128)S(1)}, f32[1,16,128]{2,1,0:T(8,128)S(1)}, u32[]{:S(2)}, u32[]{:S(2)}) collective-permute-start(f32[1,16,128]{2,1,0:T(8,128)S(1)} %get-tuple-element.21), channel_id=1, source_target_pairs={{0,8},{8,16},{16,24},{1,9},{9,17},{17,25},{2,10},{10,18},{18,26},{... | collective-permute-start | bytes 24584 | tf_op jit(solution)/shard_map/ppermute | solution.py:15
  7.7 4.5 %collective-permute-start.4 = (f32[1,16,128]{2,1,0:T(8,128)S(1)}, f32[1,16,128]{2,1,0:T(8,128)S(1)}, u32[]{:S(2)}, u32[]{:S(2)}) collective-permute-start(f32[1,16,128]{2,1,0:T(8,128)S(1)} %get-tuple-element.20), channel_id=1, source_target_pairs={{0,8},{8,16},{16,24},{1,9},{9,17},{17,25},{2,10},{10,18},{18,26},{... | collective-permute-start | bytes 24584 | tf_op jit(solution)/shard_map/ppermute | solution.py:15
  13.6 3.0 %collective-permute-start.1 = (f32[1,16,128]{2,1,0:T(8,128)S(1)}, f32[1,16,128]{2,1,0:T(8,128)S(1)}, u32[]{:S(2)}, u32[]{:S(2)}) collective-permute-start(f32[1,16,128]{2,1,0:T(8,128)S(1)} %slice.156), channel_id=1, source_target_pairs={{0,8},{8,16},{16,24},{1,9},{9,17},{17,25},{2,10},{10,18},{18,26},{... | collective-permute-start | bytes 24584 | tf_op jit(solution)/shard_map/ppermute | solution.py:15
  18.1 4.5 %collective-permute-start.7 = (f32[66,1,128]{2,1,0:T(1,128)S(1)}, f32[66,1,128]{2,1,0:T(1,128)S(1)}, u32[]{:S(2)}, u32[]{:S(2)}) collective-permute-start(f32[66,1,128]{2,1,0:T(1,128)S(1)} %get-tuple-element.18), channel_id=1, source_target_pairs={{0,1},{1,2},{2,3},{3,4},{4,5},{5,6},{6,7},{8,9},{9,10},{10,11},{11... | collective-permute-start | bytes 101384 | tf_op jit(solution)/shard_map/ppermute | solution.py:15
  22.7 4.3 %collective-permute-start.6 = (f32[66,1,128]{2,1,0:T(1,128)S(1)}, f32[66,1,128]{2,1,0:T(1,128)S(1)}, u32[]{:S(2)}, u32[]{:S(2)}) collective-permute-start(f32[66,1,128]{2,1,0:T(1,128)S(1)} %slice.194), channel_id=1, source_target_pairs={{0,1},{1,2},{2,3},{3,4},{4,5},{5,6},{6,7},{8,9},{9,10},{10,11},{11... | collective-permute-start | bytes 101384 | tf_op jit(solution)/shard_map/ppermute | solution.py:15
  27.3 1.3 collective-permute-done.6
  28.6 1.6 fusion.33
  31.5 1.4 collective-permute-start.8
  33.0 3.0 %collective-permute-start.9 = (f32[8,1,16,128]{3,0,2,1:T(8,128)S(1)}, f32[8,1,16,128]{3,0,2,1:T(8,128)S(1)}, u32[]{:S(2)}, u32[]{:S(2)}) collective-permute-start(f32[8,1,16,128]{3,0,2,1:T(8,128)S(1)} %get-tuple-element.15), channel_id=1, source_target_pairs={{0,8},{8,16},{16,24},{1,9},{9,17},{17,25},{2,10},{10,18},{18,26},{... | collective-permute-start | bytes 196616 | tf_op jit(solution)/shard_map/ppermute | solution.py:15
  38.2 5.0 %collective-permute-start.11 = (f32[8,66,1,128]{3,0,2,1:T(8,128)S(1)}, f32[8,66,1,128]{3,0,2,1:T(8,128)S(1)}, u32[]{:S(2)}, u32[]{:S(2)}) collective-permute-start(f32[8,66,1,128]{3,0,2,1:T(8,128)S(1)} %get-tuple-element.12), channel_id=1, source_target_pairs={{0,1},{1,2},{2,3},{3,4},{4,5},{5,6},{6,7},{8,9},{9,10},{10,11},{11... | collective-permute-start | bytes 811016 | tf_op jit(solution)/shard_map/ppermute | solution.py:15
  43.5 4.0 %collective-permute-done.10 = f32[8,66,1,128]{3,0,2,1:T(8,128)S(1)} collective-permute-done((f32[8,66,1,128]{3,0,2,1:T(8,128)S(1)}, f32[8,66,1,128]{3,0,2,1:T(8,128)S(1)}, u32[]{:S(2)}, u32[]{:S(2)}) %collective-permute-start.10) | collective-permute-done | bytes 270368 | tf_op jit(solution)/shard_map/ppermute | solution.py:18
  47.6 7.2 %collective-permute-done.11 = f32[8,66,1,128]{3,0,2,1:T(8,128)S(1)} collective-permute-done((f32[8,66,1,128]{3,0,2,1:T(8,128)S(1)}, f32[8,66,1,128]{3,0,2,1:T(8,128)S(1)}, u32[]{:S(2)}, u32[]{:S(2)}) %collective-permute-start.11) | collective-permute-done | bytes 270368 | tf_op jit(solution)/shard_map/ppermute | solution.py:15
  54.8 8.3 %multiply_subtract_fusion = (f32[8,64,16,128]{3,0,2,1:T(8,128)S(1)}, f32[8,64,16,128]{3,0,2,1:T(8,128)}) fusion(f32[8,64,16]{0,2,1:T(8,128)S(1)} %fusion.43, f32[64,16,128]{2,1,0:T(8,128)S(1)} %get-tuple-element.7, f32[64,16,128]{2,1,0:T(8,128)S(1)} %pad.18, f32[8,64,16,128]{3,0,2,1:T(8,128)S(1)} %broadcast_multiply_fusion, f32[64,16,128]{2,1,0:T(8,128)S(1)} %copy-done.8, ...), kind=kLoop, calls=%fused_computation.51 | loop fusion | flops 25165824 | bytes 17481728 | tf_op jit(solution)/shard_map/sub | solution.py:73
  63.1 11.2 %fusion.28 = f32[16,16]{0,1:T(8,128)S(1)} fusion(f32[8,64,16,128]{3,0,2,1:T(8,128)S(1)} %get-tuple-element.5, f32[8,64,16,128]{3,0,2,1:T(8,128)S(1)} %broadcast_multiply_fusion), kind=kOutput, calls=%fused_computation.55 | convolution fusion | flops 404750336 | bytes 8389632 | tf_op jit(solution)/shard_map/aijk,bijk->ab/dot_general | solution.py:78
  74.3 1.3 collective-permute-start.12
  75.6 3.0 %collective-permute-start.13 = (f32[8,1,16,128]{3,0,2,1:T(8,128)S(1)}, f32[8,1,16,128]{3,0,2,1:T(8,128)S(1)}, u32[]{:S(2)}, u32[]{:S(2)}) collective-permute-start(f32[8,1,16,128]{3,0,2,1:T(8,128)S(1)} %get-tuple-element.13), channel_id=1, source_target_pairs={{0,8},{8,16},{16,24},{1,9},{9,17},{17,25},{2,10},{10,18},{18,26},{... | collective-permute-start | bytes 196616 | tf_op jit(solution)/shard_map/ppermute | solution.py:15
  78.6 20.1 %psum.21 = f32[16,16]{0,1:T(8,128)S(1)} all-reduce(f32[16,16]{0,1:T(8,128)S(1)} %fusion.28), channel_id=1, replica_groups=mesh['gx'=4,'gy'=8] {'gy'}, use_global_device_ids=true, to_apply=%region_1.2 | all-reduce | flops 256 | bytes 2048 | tf_op jit(solution)/shard_map/psum | solution.py:80
  98.8 5.8 %psum.22 = f32[16,16]{0,1:T(8,128)S(1)} all-reduce(f32[16,16]{0,1:T(8,128)S(1)} %psum.21), channel_id=1, replica_groups=mesh['gx'=4,'gy'=8] {'gx'}, use_global_device_ids=true, to_apply=%region_2.3 | all-reduce | flops 256 | bytes 2048 | tf_op jit(solution)/shard_map/psum | solution.py:80
  104.6 1.5 cholesky.44
  109.9 1.6 collective-permute-start.14
  111.5 4.6 %collective-permute-start.15 = (f32[8,66,1,128]{3,0,2,1:T(8,128)S(1)}, f32[8,66,1,128]{3,0,2,1:T(8,128)S(1)}, u32[]{:S(2)}, u32[]{:S(2)}) collective-permute-start(f32[8,66,1,128]{3,0,2,1:T(8,128)S(1)} %get-tuple-element.10), channel_id=1, source_target_pairs={{0,1},{1,2},{2,3},{3,4},{4,5},{5,6},{6,7},{8,9},{9,10},{10,11},{11... | collective-permute-start | bytes 811016 | tf_op jit(solution)/shard_map/ppermute | solution.py:15
  116.4 3.7 %collective-permute-done.14 = f32[8,66,1,128]{3,0,2,1:T(8,128)S(1)} collective-permute-done((f32[8,66,1,128]{3,0,2,1:T(8,128)S(1)}, f32[8,66,1,128]{3,0,2,1:T(8,128)S(1)}, u32[]{:S(2)}, u32[]{:S(2)}) %collective-permute-start.14) | collective-permute-done | bytes 270368 | tf_op jit(solution)/shard_map/ppermute | solution.py:18
  120.1 3.6 %collective-permute-done.15 = f32[8,66,1,128]{3,0,2,1:T(8,128)S(1)} collective-permute-done((f32[8,66,1,128]{3,0,2,1:T(8,128)S(1)}, f32[8,66,1,128]{3,0,2,1:T(8,128)S(1)}, u32[]{:S(2)}, u32[]{:S(2)}) %collective-permute-start.15) | collective-permute-done | bytes 270368 | tf_op jit(solution)/shard_map/ppermute | solution.py:15
  123.7 7.9 %fusion.10 = f32[8,64,16,128]{3,0,2,1:T(8,128)S(1)} fusion(f32[8,64,16,128]{3,0,2,1:T(8,128)S(1)} %copy-done.4, f32[8,66,1,128]{3,0,2,1:T(8,128)S(1)} %collective-permute-done.15, f32[8,1,16,128]{3,0,2,1:T(8,128)S(1)} %collective-permute-done.12, f32[8,1,16,128]{3,0,2,1:T(8,128)S(1)} %collective-permute-done.13, ...), kind=kLoop, calls=%fused_computation.16 | loop fusion | flops 22020096 | bytes 12730368 | tf_op jit(solution)/shard_map/sub | solution.py:39
  131.6 2.0 copy-done.7
  133.5 10.6 %fusion.29 = f32[16,16]{1,0:T(8,128)S(1)} fusion(f32[8,64,16,128]{3,0,2,1:T(8,128)S(1)} %fusion.10, f32[8,64,16,128]{3,0,2,1:T(8,128)S(1)} %copy-done.6, f32[8,64,16,128]{3,0,2,1:T(8,128)S(1)} %copy-done.4, f32[8,64,16,128]{3,0,2,1:T(8,128)S(1)} %copy-done.1), kind=kOutput, calls=%fused_computation.56 | convolution fusion | flops 406847488 | bytes 16778240 | tf_op jit(solution)/shard_map/aijk,bijk->ab/dot_general | solution.py:79
  144.2 38.9 %psum.23 = f32[16,16]{1,0:T(8,128)S(1)} all-reduce(f32[16,16]{1,0:T(8,128)S(1)} %fusion.29), channel_id=1, replica_groups=mesh['gx'=4,'gy'=8] {'gx','gy'}, use_global_device_ids=true, to_apply=%region_5.7 | all-reduce | flops 256 | bytes 2048 | tf_op jit(solution)/shard_map/psum | solution.py:81
  183.5 1.5 cholesky.55
  188.1 6.6 %fusion = f32[1,64,16,128]{3,0,2,1:T(1,128)S(1)} fusion(f32[8,64,16,128]{3,0,2,1:T(8,128)} %copy-done.7, f32[8,64,16,128]{3,0,2,1:T(8,128)} %get-tuple-element.6, f32[16]{0:T(128)S(1)} %get-tuple-element.23), kind=kOutput, calls=%fused_computation.6 | convolution fusion | flops 27262976 | bytes 8912960 | tf_op jit(solution)/shard_map/a,aijk->ijk/dot_general | solution.py:85
  195.6 8.6 %copy_add_fusion = f32[8,64,16,128]{3,0,2,1:T(8,128)S(1)} fusion(f32[8,64,16,128]{3,2,1,0:T(8,128)} %param.13, f32[8,64,16,128]{3,0,2,1:T(8,128)S(1)} %copy-done.5, f32[8,64,16,128]{3,0,2,1:T(8,128)S(1)} %copy-done.2, f32[16,8]{0,1:T(8,128)S(1)} %get-tuple-element.24), kind=kOutput, calls=%fused_computation.50 | convolution fusion | flops 204472320 | bytes 16777728 | tf_op jit(solution)/shard_map/ab,aijk->bijk/dot_general | solution.py:83
  204.2 2.8 %copy.15 = f32[8,64,16,128]{3,2,1,0:T(8,128)} copy(f32[8,64,16,128]{3,0,2,1:T(8,128)S(1)} %copy_add_fusion) | data formatting | bytes 8388608
  (85 shorter events, 16.7 us)
Async XLA Ops:
  0.6 7.1 %copy-start.9 = (f32[64,16,128]{2,1,0:T(8,128)S(1)}, f32[64,16,128]{2,1,0:T(8,128)}, u32[]{:S(2)}) copy-start(f32[64,16,128]{2,1,0:T(8,128)} %param.11) | copy-start | bytes 1572868
  0.6 12.9 %copy-start.10 = (f32[64,16,128]{2,1,0:T(8,128)S(1)}, f32[64,16,128]{2,1,0:T(8,128)}, u32[]{:S(2)}) copy-start(f32[64,16,128]{2,1,0:T(8,128)} %param.10) | copy-start | bytes 1572868
  0.7 16.0 %copy-start.15 = (s32[64,16]{0,1:T(8,128)S(1)}, s32[64,16]{0,1:T(8,128)}, u32[]{:S(2)}) copy-start(s32[64,16]{0,1:T(8,128)} %param.14) | copy-start | bytes 12292
  0.7 28.0 %copy-start.8 = (f32[64,16,128]{2,1,0:T(8,128)S(1)}, f32[64,16,128]{2,1,0:T(8,128)}, u32[]{:S(2)}) copy-start(f32[64,16,128]{2,1,0:T(8,128)} %param.12) | copy-start | bytes 1572868
  0.7 28.0 %copy-start.11 = (f32[64,16,128]{2,1,0:T(8,128)S(1)}, f32[64,16,128]{2,1,0:T(8,128)}, u32[]{:S(2)}) copy-start(f32[64,16,128]{2,1,0:T(8,128)} %param.9) | copy-start | bytes 1572868
  3.4 13.3 %collective-permute-start = (f32[1,16,128]{2,1,0:T(8,128)S(1)}, f32[1,16,128]{2,1,0:T(8,128)S(1)}, u32[]{:S(2)}, u32[]{:S(2)}) collective-permute-start(f32[1,16,128]{2,1,0:T(8,128)S(1)} %get-tuple-element.22), channel_id=1, source_target_pairs={{8,0},{16,8},{24,16},{9,1},{17,9},{25,17},{10,2},{18,10},{26,18},{... | collective-permute-start | bytes 24584 | tf_op jit(solution)/shard_map/ppermute | solution.py:18
  4.7 12.0 %collective-permute-start.2 = (f32[1,16,128]{2,1,0:T(8,128)S(1)}, f32[1,16,128]{2,1,0:T(8,128)S(1)}, u32[]{:S(2)}, u32[]{:S(2)}) collective-permute-start(f32[1,16,128]{2,1,0:T(8,128)S(1)} %get-tuple-element.21), channel_id=1, source_target_pairs={{0,8},{8,16},{16,24},{1,9},{9,17},{17,25},{2,10},{10,18},{18,26},{... | collective-permute-start | bytes 24584 | tf_op jit(solution)/shard_map/ppermute | solution.py:15
  7.7 14.9 %collective-permute-start.4 = (f32[1,16,128]{2,1,0:T(8,128)S(1)}, f32[1,16,128]{2,1,0:T(8,128)S(1)}, u32[]{:S(2)}, u32[]{:S(2)}) collective-permute-start(f32[1,16,128]{2,1,0:T(8,128)S(1)} %get-tuple-element.20), channel_id=1, source_target_pairs={{0,8},{8,16},{16,24},{1,9},{9,17},{17,25},{2,10},{10,18},{18,26},{... | collective-permute-start | bytes 24584 | tf_op jit(solution)/shard_map/ppermute | solution.py:15
  12.2 10.4 %collective-permute-start.5 = (f32[1,16,128]{2,1,0:T(8,128)S(1)}, f32[1,16,128]{2,1,0:T(8,128)S(1)}, u32[]{:S(2)}, u32[]{:S(2)}) collective-permute-start(f32[1,16,128]{2,1,0:T(8,128)S(1)} %get-tuple-element.19), channel_id=1, source_target_pairs={{8,0},{16,8},{24,16},{9,1},{17,9},{25,17},{10,2},{18,10},{26,18},{... | collective-permute-start | bytes 24584 | tf_op jit(solution)/shard_map/ppermute | solution.py:18
  13.6 13.7 %collective-permute-start.1 = (f32[1,16,128]{2,1,0:T(8,128)S(1)}, f32[1,16,128]{2,1,0:T(8,128)S(1)}, u32[]{:S(2)}, u32[]{:S(2)}) collective-permute-start(f32[1,16,128]{2,1,0:T(8,128)S(1)} %slice.156), channel_id=1, source_target_pairs={{0,8},{8,16},{16,24},{1,9},{9,17},{17,25},{2,10},{10,18},{18,26},{... | collective-permute-start | bytes 24584 | tf_op jit(solution)/shard_map/ppermute | solution.py:15
  16.8 10.5 %collective-permute-start.3 = (f32[66,1,128]{2,1,0:T(1,128)S(1)}, f32[66,1,128]{2,1,0:T(1,128)S(1)}, u32[]{:S(2)}, u32[]{:S(2)}) collective-permute-start(f32[66,1,128]{2,1,0:T(1,128)S(1)} %get-tuple-element.17), channel_id=1, source_target_pairs={{1,0},{2,1},{3,2},{4,3},{5,4},{6,5},{7,6},{9,8},{10,9},{11,10},{12... | collective-permute-start | bytes 101384 | tf_op jit(solution)/shard_map/ppermute | solution.py:18
  18.1 9.2 %collective-permute-start.7 = (f32[66,1,128]{2,1,0:T(1,128)S(1)}, f32[66,1,128]{2,1,0:T(1,128)S(1)}, u32[]{:S(2)}, u32[]{:S(2)}) collective-permute-start(f32[66,1,128]{2,1,0:T(1,128)S(1)} %get-tuple-element.18), channel_id=1, source_target_pairs={{0,1},{1,2},{2,3},{3,4},{4,5},{5,6},{6,7},{8,9},{9,10},{10,11},{11... | collective-permute-start | bytes 101384 | tf_op jit(solution)/shard_map/ppermute | solution.py:15
  22.7 5.9 %collective-permute-start.6 = (f32[66,1,128]{2,1,0:T(1,128)S(1)}, f32[66,1,128]{2,1,0:T(1,128)S(1)}, u32[]{:S(2)}, u32[]{:S(2)}) collective-permute-start(f32[66,1,128]{2,1,0:T(1,128)S(1)} %slice.194), channel_id=1, source_target_pairs={{0,1},{1,2},{2,3},{3,4},{4,5},{5,6},{6,7},{8,9},{9,10},{10,11},{11... | collective-permute-start | bytes 101384 | tf_op jit(solution)/shard_map/ppermute | solution.py:15
  30.2 24.6 %copy-start.14 = (f32[64,16,128]{2,1,0:T(8,128)}, f32[64,16,128]{2,1,0:T(8,128)S(1)}, u32[]{:S(2)}) copy-start(f32[64,16,128]{2,1,0:T(8,128)S(1)} %get-tuple-element.8) | copy-start | bytes 1572868
  31.5 31.6 %copy-start = (f32[8,64,16,128]{3,0,2,1:T(8,128)}, f32[8,64,16,128]{3,0,2,1:T(8,128)S(1)}, u32[]{:S(2)}) copy-start(f32[8,64,16,128]{3,0,2,1:T(8,128)S(1)} %broadcast_multiply_fusion) | copy-start | bytes 12582916
  31.5 23.3 %copy-start.12 = (f32[64,16,128]{2,1,0:T(8,128)S(1)}, f32[64,16,128]{2,1,0:T(8,128)}, u32[]{:S(2)}) copy-start(f32[64,16,128]{2,1,0:T(8,128)} %param.9) | copy-start | bytes 1572868
  31.5 4.5 %collective-permute-start.8 = (f32[8,1,16,128]{3,0,2,1:T(8,128)S(1)}, f32[8,1,16,128]{3,0,2,1:T(8,128)S(1)}, u32[]{:S(2)}, u32[]{:S(2)}) collective-permute-start(f32[8,1,16,128]{3,0,2,1:T(8,128)S(1)} %get-tuple-element.16), channel_id=1, source_target_pairs={{8,0},{16,8},{24,16},{9,1},{17,9},{25,17},{10,2},{18,10},{26,18},{... | collective-permute-start | bytes 196616 | tf_op jit(solution)/shard_map/ppermute | solution.py:18
  33.0 3.9 %collective-permute-start.9 = (f32[8,1,16,128]{3,0,2,1:T(8,128)S(1)}, f32[8,1,16,128]{3,0,2,1:T(8,128)S(1)}, u32[]{:S(2)}, u32[]{:S(2)}) collective-permute-start(f32[8,1,16,128]{3,0,2,1:T(8,128)S(1)} %get-tuple-element.15), channel_id=1, source_target_pairs={{0,8},{8,16},{16,24},{1,9},{9,17},{17,25},{2,10},{10,18},{18,26},{... | collective-permute-start | bytes 196616 | tf_op jit(solution)/shard_map/ppermute | solution.py:15
  36.9 10.6 %collective-permute-start.10 = (f32[8,66,1,128]{3,0,2,1:T(8,128)S(1)}, f32[8,66,1,128]{3,0,2,1:T(8,128)S(1)}, u32[]{:S(2)}, u32[]{:S(2)}) collective-permute-start(f32[8,66,1,128]{3,0,2,1:T(8,128)S(1)} %get-tuple-element.11), channel_id=1, source_target_pairs={{1,0},{2,1},{3,2},{4,3},{5,4},{6,5},{7,6},{9,8},{10,9},{11,10},{12... | collective-permute-start | bytes 811016 | tf_op jit(solution)/shard_map/ppermute | solution.py:18
  38.2 16.6 %collective-permute-start.11 = (f32[8,66,1,128]{3,0,2,1:T(8,128)S(1)}, f32[8,66,1,128]{3,0,2,1:T(8,128)S(1)}, u32[]{:S(2)}, u32[]{:S(2)}) collective-permute-start(f32[8,66,1,128]{3,0,2,1:T(8,128)S(1)} %get-tuple-element.12), channel_id=1, source_target_pairs={{0,1},{1,2},{2,3},{3,4},{4,5},{5,6},{6,7},{8,9},{9,10},{10,11},{11... | collective-permute-start | bytes 811016 | tf_op jit(solution)/shard_map/ppermute | solution.py:15
  63.1 11.2 %copy-start.3 = (f32[8,64,16,128]{3,0,2,1:T(8,128)}, f32[8,64,16,128]{3,0,2,1:T(8,128)S(1)}, u32[]{:S(2)}) copy-start(f32[8,64,16,128]{3,0,2,1:T(8,128)S(1)} %get-tuple-element.5) | copy-start | bytes 12582916
  74.3 34.3 %collective-permute-start.12 = (f32[8,1,16,128]{3,0,2,1:T(8,128)S(1)}, f32[8,1,16,128]{3,0,2,1:T(8,128)S(1)}, u32[]{:S(2)}, u32[]{:S(2)}) collective-permute-start(f32[8,1,16,128]{3,0,2,1:T(8,128)S(1)} %get-tuple-element.14), channel_id=1, source_target_pairs={{8,0},{16,8},{24,16},{9,1},{17,9},{25,17},{10,2},{18,10},{26,18},{... | collective-permute-start | bytes 196616 | tf_op jit(solution)/shard_map/ppermute | solution.py:18
  75.6 33.0 %collective-permute-start.13 = (f32[8,1,16,128]{3,0,2,1:T(8,128)S(1)}, f32[8,1,16,128]{3,0,2,1:T(8,128)S(1)}, u32[]{:S(2)}, u32[]{:S(2)}) collective-permute-start(f32[8,1,16,128]{3,0,2,1:T(8,128)S(1)} %get-tuple-element.13), channel_id=1, source_target_pairs={{0,8},{8,16},{16,24},{1,9},{9,17},{17,25},{2,10},{10,18},{18,26},{... | collective-permute-start | bytes 196616 | tf_op jit(solution)/shard_map/ppermute | solution.py:15
  108.6 15.1 %copy-start.4 = (f32[8,64,16,128]{3,0,2,1:T(8,128)S(1)}, f32[8,64,16,128]{3,0,2,1:T(8,128)}, u32[]{:S(2)}) copy-start(f32[8,64,16,128]{3,0,2,1:T(8,128)} %copy-done.3) | copy-start | bytes 12582916
  108.6 15.1 %copy-start.13 = (f32[64,16,128]{2,1,0:T(8,128)S(1)}, f32[64,16,128]{2,1,0:T(8,128)}, u32[]{:S(2)}) copy-start(f32[64,16,128]{2,1,0:T(8,128)} %param.9) | copy-start | bytes 1572868
  109.9 10.2 %collective-permute-start.14 = (f32[8,66,1,128]{3,0,2,1:T(8,128)S(1)}, f32[8,66,1,128]{3,0,2,1:T(8,128)S(1)}, u32[]{:S(2)}, u32[]{:S(2)}) collective-permute-start(f32[8,66,1,128]{3,0,2,1:T(8,128)S(1)} %get-tuple-element.9), channel_id=1, source_target_pairs={{1,0},{2,1},{3,2},{4,3},{5,4},{6,5},{7,6},{9,8},{10,9},{11,10},{12... | collective-permute-start | bytes 811016 | tf_op jit(solution)/shard_map/ppermute | solution.py:18
  111.5 12.2 %collective-permute-start.15 = (f32[8,66,1,128]{3,0,2,1:T(8,128)S(1)}, f32[8,66,1,128]{3,0,2,1:T(8,128)S(1)}, u32[]{:S(2)}, u32[]{:S(2)}) collective-permute-start(f32[8,66,1,128]{3,0,2,1:T(8,128)S(1)} %get-tuple-element.10), channel_id=1, source_target_pairs={{0,1},{1,2},{2,3},{3,4},{4,5},{5,6},{6,7},{8,9},{9,10},{10,11},{11... | collective-permute-start | bytes 811016 | tf_op jit(solution)/shard_map/ppermute | solution.py:15
  116.4 17.2 %copy-start.1 = (f32[8,64,16,128]{3,0,2,1:T(8,128)S(1)}, f32[8,64,16,128]{3,0,2,1:T(8,128)}, u32[]{:S(2)}) copy-start(f32[8,64,16,128]{3,0,2,1:T(8,128)} %copy-done) | copy-start | bytes 12582916
  116.4 17.2 %copy-start.6 = (f32[8,64,16,128]{3,0,2,1:T(8,128)S(1)}, f32[8,64,16,128]{3,0,2,1:T(8,128)}, u32[]{:S(2)}) copy-start(f32[8,64,16,128]{3,0,2,1:T(8,128)} %get-tuple-element.6) | copy-start | bytes 12582916
  131.6 2.0 copy-start.7
  188.1 7.5 %copy-start.2 = (f32[8,64,16,128]{3,0,2,1:T(8,128)S(1)}, f32[8,64,16,128]{3,0,2,1:T(8,128)}, u32[]{:S(2)}) copy-start(f32[8,64,16,128]{3,0,2,1:T(8,128)} %copy-done) | copy-start | bytes 12582916
  188.1 7.5 %copy-start.5 = (f32[8,64,16,128]{3,0,2,1:T(8,128)S(1)}, f32[8,64,16,128]{3,0,2,1:T(8,128)}, u32[]{:S(2)}) copy-start(f32[8,64,16,128]{3,0,2,1:T(8,128)} %copy-done.3) | copy-start | bytes 12582916
